TPU v7x, 128 devices: a whole 4x4x4 slice. The times are simulated.
128 devices in a mesh: node: 32 (over y_hi, z, x), query: 4 (over y_lo, core).
Axes of the slice: x: 4, y: 4 (y_hi: 2, y_lo: 2; y = y_hi * 2 + y_lo), z: 4, core: 2. Of those that a mesh axis runs over, the one named last changes fastest.
Arguments:
- entity_state: bfloat16 [32768, 2048], P('node', 'query'), may hold values from -6 to 6
- edge_tiles: int32 [512, 3, 512], P('node'), may hold values from 0 to 4095, as said below
- query_head: int32 [64], P('query'), may hold values from 0 to 32767
- query_relation: int32 [64], P('query'), may hold values from 0 to 821
- query_table: float32 [822, 32], replicated, may hold values from -6 to 6
- rel_vectors: float32 [2, 822, 32], replicated, may hold values from -1.8 to 1.8
- mix_weight: float32 [2, 32, 32], replicated, may hold values from -1 to 1
- mix_bias: float32 [2, 32], replicated, may hold values from -3 to 3
- cotangent: bfloat16 [32768, 2048], P('node', 'query'), may hold values from -6 to 6
Outputs:
- final_state: bfloat16 [32768, 2048], P('node', 'query')
- weight_grads: float32 [2, 32, 32], replicated
- bias_grads: float32 [2, 32], replicated
Inputs may be any that keep to these rules, and one draw needn't show every extreme that they name: edge_tiles[t,0,:] lies in 0 to 4095, edge_tiles[t,1,:] in 0 to 63, edge_tiles[t,2,:] in 0 to 821.
All inputs are finite; a program needn't handle non-finite values.
Results may differ from a plain program's by a relative error of at most 0.0056.
Values may be sent and summed in bfloat16 or wider, within the bound.
A program may use at most 192 MiB of HBM per device.

v0:
```python
import jax
import jax.numpy as jnp
from jax import lax
from jax.sharding import PartitionSpec as P

DIM = 32


def with_halo(block, sides, width):
    for axis, dim in sides:
        count = lax.axis_size(axis)
        forward = [(i, i + 1) for i in range(count - 1)]
        forward.append((count - 1, 0))
        backward = [(target, source) for source, target in forward]
        low = lax.ppermute(
            lax.slice_in_dim(block, block.shape[dim] - width, None, axis=dim), axis, forward
        )
        high = lax.ppermute(lax.slice_in_dim(block, 0, width, axis=dim), axis, backward)
        block = jnp.concatenate([low, block, high], axis=dim)
    return block


def from_partner(block, axis, apart):
    count = lax.axis_size(axis)
    route = []
    for low in range(count):
        high = low | 1 << apart
        if high != low and high < count:
            route += [(low, high), (high, low)]
    return lax.ppermute(block, axis, route)


def passed_along(block, axis, distance):
    devices = range(lax.axis_size(axis))
    route = [((i - distance) % len(devices), i) for i in devices]
    return lax.ppermute(block, axis, route)


def silu_slope(values):
    sigma = jax.nn.sigmoid(values)
    return sigma * (1.0 + values * (1.0 - sigma))


def target_onehot(edge_block):
    return (edge_block[:, 1, :][:, None, :] == lax.iota(jnp.int32, 64)[None, :, None]).astype(
        jnp.bfloat16
    )


def contributions(grad_panel, edge_block, dst_onehot, rel_table, slot_base, slot_count):
    tile_count = edge_block.shape[0]
    slot_total = edge_block.shape[2]
    col_count = grad_panel.shape[1]
    per_edge = jnp.einsum(
        "tre,trc->tec",
        dst_onehot,
        grad_panel.reshape(tile_count, 64, col_count),
        preferred_element_type=jnp.float32,
    )
    rel_scales = jnp.take(rel_table, edge_block[:, 2, :], axis=0)
    edge_terms = (
        per_edge.reshape(tile_count, slot_total, col_count // DIM, DIM) * rel_scales[:, :, None, :]
    ).reshape(tile_count * slot_total, col_count)
    segment_ids = edge_block[:, 0, :].reshape(-1) - slot_base
    segment_ids = jnp.where(
        (segment_ids >= 0) & (segment_ids < slot_count), segment_ids, slot_count
    )
    summed = jax.ops.segment_sum(edge_terms, segment_ids, num_segments=slot_count + 1)
    return summed[:slot_count]


def reduce_grads(values):
    return lax.psum((values[0], values[1]), ("node", "query"))


def body(
    entity_state,
    edge_tiles,
    query_head,
    query_relation,
    query_table,
    rel_vectors,
    mix_weight,
    mix_bias,
    cotangent,
):
    highest = lax.Precision.HIGHEST
    row_count = entity_state.shape[0]
    tile_count = edge_tiles.shape[0]
    slot_total = edge_tiles.shape[2]
    query_count = query_head.shape[0]
    col_count = query_count * DIM
    mirror_bit = lax.axis_size("node").bit_length() - 2
    first_row = lax.axis_index("node") * row_count
    entity_ids = first_row + lax.iota(jnp.int32, row_count)
    choose_rel = (
        query_relation[:, None] == lax.iota(jnp.int32, query_table.shape[0])[None, :]
    ).astype(jnp.float32)
    query_vec = jnp.dot(
        choose_rel, query_table, precision=highest, preferred_element_type=jnp.float32
    )
    head_match = (entity_ids[:, None] == query_head[None, :]).astype(jnp.float32)
    boundary = (
        (head_match[:, :, None] * query_vec[None, :, :])
        .reshape(row_count, col_count)
        .astype(jnp.bfloat16)
    )
    own_onehot = target_onehot(edge_tiles)

    def window(state_panel):
        sides = with_halo(state_panel, (("node", 0),), row_count)
        mirror = from_partner(state_panel, "node", mirror_bit)
        return jnp.concatenate([sides, mirror], axis=0)

    def run_layer(state_panel, layer_index):
        extended = window(state_panel)
        gathered = jnp.take(extended, edge_tiles[:, 0, :], axis=0)
        rel_scales = jnp.take(rel_vectors[layer_index], edge_tiles[:, 2, :], axis=0)
        message = (
            gathered.reshape(tile_count, slot_total, query_count, DIM) * rel_scales[:, :, None, :]
        ).astype(jnp.bfloat16)
        message = message.reshape(tile_count, slot_total, col_count)
        summed = jnp.einsum(
            "tre,tec->trc", own_onehot, message, preferred_element_type=jnp.float32
        ).reshape(row_count, col_count)
        mixed_in = boundary.astype(jnp.float32) + summed
        update = (
            jnp.einsum(
                "rqd,de->rqe",
                mixed_in.reshape(row_count, query_count, DIM),
                mix_weight[layer_index],
                precision=highest,
            )
            + mix_bias[layer_index]
        )
        result = (
            state_panel.astype(jnp.float32) + jax.nn.silu(update).reshape(row_count, col_count)
        ).astype(jnp.bfloat16)
        return (mixed_in, update, result)

    mixed_zero, update_zero, state_one = run_layer(entity_state, 0)
    mixed_one, update_one, state_two = run_layer(state_one, 1)
    grad_out = cotangent.astype(jnp.float32)
    grad_update_one = grad_out.reshape(row_count, query_count, DIM) * silu_slope(update_one)
    weight_one = jnp.einsum(
        "rqd,rqe->de",
        mixed_one.reshape(row_count, query_count, DIM),
        grad_update_one,
        precision=highest,
    )
    bias_one = jnp.sum(grad_update_one, axis=(0, 1))
    weight_one, bias_one = reduce_grads((weight_one, bias_one))
    grad_mixed_one = (
        jnp.einsum("rqe,de->rqd", grad_update_one, mix_weight[1], precision=highest)
        .reshape(row_count, col_count)
        .astype(jnp.bfloat16)
    )
    window_terms = contributions(
        grad_mixed_one, edge_tiles, own_onehot, rel_vectors[1], 0, 4 * row_count
    )
    own_terms = window_terms[row_count : 2 * row_count]
    back_right = passed_along(window_terms[:row_count].astype(jnp.bfloat16), "node", -1)
    back_left = passed_along(
        window_terms[2 * row_count : 3 * row_count].astype(jnp.bfloat16), "node", 1
    )
    back_mirror = from_partner(
        window_terms[3 * row_count :].astype(jnp.bfloat16), "node", mirror_bit
    )
    adjoint_sum = (
        own_terms
        + back_right.astype(jnp.float32)
        + back_left.astype(jnp.float32)
        + back_mirror.astype(jnp.float32)
    )
    grad_state_one = grad_out + adjoint_sum
    grad_update_zero = grad_state_one.reshape(row_count, query_count, DIM) * silu_slope(update_zero)
    weight_zero = jnp.einsum(
        "rqd,rqe->de",
        mixed_zero.reshape(row_count, query_count, DIM),
        grad_update_zero,
        precision=highest,
    )
    bias_zero = jnp.sum(grad_update_zero, axis=(0, 1))
    weight_zero, bias_zero = reduce_grads((weight_zero, bias_zero))
    weight_grads = jnp.stack([weight_zero, weight_one])
    bias_grads = jnp.stack([bias_zero, bias_one])
    return (state_two, weight_grads, bias_grads)


def solution(mesh):
    placed = (
        P("node", "query"),
        P("node", None, None),
        P("query"),
        P("query"),
        P(),
        P(),
        P(),
        P(),
        P("node", "query"),
    )
    return jax.shard_map(
        body, mesh=mesh, in_specs=placed, out_specs=(P("node", "query"), P(), P()), check_vma=False
    )
```

profile of v0, /device:TPU:1, one launch (start us, length us, event | category | flops | bytes accessed | tf_op | source)
XLA Modules:
  0.0 584.9 jit_solution(341249885668741540)
XLA Ops:
  0.6 9.5 %collective-permute-start.1 = (bf16[1024,512]{1,0:T(8,128)(2,1)}, bf16[1024,512]{1,0:T(8,128)(2,1)}, u32[]{:S(2)}, u32[]{:S(2)}) collective-permute-start(bf16[1024,512]{1,0:T(8,128)(2,1)} %param.13), channel_id=1, source_target_pairs={{4,0},{8,4},{12,8},{16,12},{20,16},{24,20},{28,24},{32,28},{36,32}... | collective-permute-start | bytes 3145736 | tf_op jit(solution)/shard_map/ppermute | solution.py:18
  13.2 27.8 %gather_fusion.1 = f32[8192,32]{1,0:T(8,128)} fusion(f32[822,32]{1,0:T(8,128)S(1)} %bitcast.102, s32[8192]{0:T(1024)S(1)} %broadcast_clamp_fusion), kind=kCustom, calls=%fused_computation.1.clone | custom fusion | bytes 2129920 | tf_op jit(solution)/shard_map/jit(_take)/gather | solution.py:118
  40.9 27.7 %gather_fusion.3 = f32[8192,32]{1,0:T(8,128)} fusion(f32[822,32]{1,0:T(8,128)S(1)} %bitcast.101, s32[8192]{0:T(1024)S(1)} %broadcast_clamp_fusion), kind=kCustom, calls=%fused_computation.3.clone | custom fusion | bytes 2129920 | tf_op jit(solution)/shard_map/jit(_take)/gather | solution.py:118
  68.7 7.5 %broadcast_select_fusion = (f32[16,512,32]{2,1,0:T(8,128)}, f32[16,512,32]{2,1,0:T(8,128)}) fusion(f32[16,512,32]{2,1,0:T(8,128)} %bitcast.109, pred[16,512]{1,0:T(8,128)(4,1)S(1)} %get-tuple-element.22, f32[16,512,32]{2,1,0:T(8,128)} %bitcast.108), kind=kLoop, calls=%fused_computation.25 | loop fusion | flops 524288 | bytes 4202496 | tf_op jit(solution)/shard_map/jit(_take)/select_n | solution.py:118
  99.3 17.7 %copy.64 = f32[64,8,16,512]{3,1,2,0:T(8,128)} copy(f32[64,8,16,512]{3,2,1,0:T(8,128)S(1)} %bitcast.105) | data formatting | bytes 33554432
  120.6 36.5 %gather_fusion = bf16[8192,512]{1,0:T(8,128)(2,1)} fusion(bf16[4096,512]{1,0:T(8,128)(2,1)} %pad_maximum_fusion, s32[8192]{0:T(1024)S(1)} %broadcast_clamp_fusion.1), kind=kCustom, calls=%fused_computation.clone | custom fusion | bytes 16809984 | tf_op jit(solution)/shard_map/jit(_take)/gather | solution.py:117
  157.1 12.4 %copy.28 = bf16[16,512,512]{1,2,0:T(8,128)(2,1)} copy(bf16[16,512,512]{2,1,0:T(8,128)(2,1)} %bitcast.107) | data formatting | bytes 16777216 | tf_op jit(solution)/shard_map/jit(_take)/gather | solution.py:117
  169.5 9.7 %fusion.1 = bf16[16,512,512]{1,2,0:T(8,128)(2,1)} fusion(bf16[16,512,512]{1,2,0:T(8,128)(2,1)} %copy.28, f32[16,512,32]{1,2,0:T(8,128)} %copy.30, pred[16,512]{1,0:T(8,128)(4,1)S(1)} %get-tuple-element.21), kind=kLoop, calls=%fused_computation.8 | loop fusion | flops 16777216 | bytes 17833984 | tf_op jit(solution)/shard_map/convert_element_type | solution.py:121
  179.2 8.0 %convert_add_fusion.3 = (f32[16,64,512]{2,1,0:T(8,128)}, f32[16,64,512]{2,1,0:T(8,128)}) fusion(f32[16,64,512]{2,1,0:T(8,128)S(1)} %copy.27, f32[512]{0:T(512)S(1)} %mul.88, bf16[16,512,512]{1,2,0:T(8,128)(2,1)} %fusion.1, s32[16,512]{1,0:T(8,128)S(1)} %get-tuple-element.20), kind=kOutput, calls=%fused_computation.16 | convolution fusion | flops 539492352 | bytes 14714880 | tf_op jit(solution)/shard_map/tre,tec->trc/dot_general | solution.py:123
  197.0 5.9 %fusion.12 = (f32[1024,16,32]{0,2,1:T(8,128)}, f32[1024,16,32]{0,2,1:T(8,128)}) fusion(f32[32]{0:T(128)S(1)} %get-tuple-element.28, f32[1024,16,32]{0,2,1:T(8,128)} %add.106, f32[2,32,32]{2,1,0:T(8,128)S(1)} %copy-done.15), kind=kOutput, calls=%fused_computation.35 | convolution fusion | flops 203948032 | bytes 6308352 | tf_op jit(solution)/shard_map/rqd,de->rqe/dot_general | solution.py:128
  210.9 7.2 %collective-permute-start.4 = (bf16[1024,512]{1,0:T(8,128)(2,1)S(1)}, bf16[1024,512]{1,0:T(8,128)(2,1)S(1)}, u32[]{:S(2)}, u32[]{:S(2)}) collective-permute-start(bf16[1024,512]{1,0:T(8,128)(2,1)S(1)} %add_convert_fusion.1), channel_id=1, source_target_pairs={{4,0},{8,4},{12,8},{16,12},{20,16},{24,20},{28,24},{32,28},{36,32}... | collective-permute-start | bytes 3145736 | tf_op jit(solution)/shard_map/ppermute | solution.py:18
  218.2 14.8 %collective-permute-done.5 = bf16[1024,512]{1,0:T(8,128)(2,1)S(1)} collective-permute-done((bf16[1024,512]{1,0:T(8,128)(2,1)S(1)}, bf16[1024,512]{1,0:T(8,128)(2,1)S(1)}, u32[]{:S(2)}, u32[]{:S(2)}) %collective-permute-start.5) | collective-permute-done | bytes 1048608 | tf_op jit(solution)/shard_map/ppermute | solution.py:30
  232.9 5.9 %collective-permute-done.4 = bf16[1024,512]{1,0:T(8,128)(2,1)S(1)} collective-permute-done((bf16[1024,512]{1,0:T(8,128)(2,1)S(1)}, bf16[1024,512]{1,0:T(8,128)(2,1)S(1)}, u32[]{:S(2)}, u32[]{:S(2)}) %collective-permute-start.4) | collective-permute-done | bytes 1048608 | tf_op jit(solution)/shard_map/ppermute | solution.py:18
  238.9 7.6 %collective-permute-done.3 = bf16[1024,512]{1,0:T(8,128)(2,1)S(1)} collective-permute-done((bf16[1024,512]{1,0:T(8,128)(2,1)S(1)}, bf16[1024,512]{1,0:T(8,128)(2,1)S(1)}, u32[]{:S(2)}, u32[]{:S(2)}) %collective-permute-start.3) | collective-permute-done | bytes 1048608 | tf_op jit(solution)/shard_map/ppermute | solution.py:15
  248.9 36.5 %gather_fusion.2 = bf16[8192,512]{1,0:T(8,128)(2,1)} fusion(bf16[4096,512]{1,0:T(8,128)(2,1)} %pad_maximum_fusion.1, s32[8192]{0:T(1024)S(1)} %broadcast_clamp_fusion.1), kind=kCustom, calls=%fused_computation.2.clone | custom fusion | bytes 16809984 | tf_op jit(solution)/shard_map/jit(_take)/gather | solution.py:117
  285.4 12.3 %copy.35 = bf16[16,512,512]{1,2,0:T(8,128)(2,1)} copy(bf16[16,512,512]{2,1,0:T(8,128)(2,1)} %bitcast.106) | data formatting | bytes 16777216 | tf_op jit(solution)/shard_map/jit(_take)/gather | solution.py:117
  297.7 9.7 %fusion = bf16[16,512,512]{1,2,0:T(8,128)(2,1)} fusion(bf16[16,512,512]{1,2,0:T(8,128)(2,1)} %copy.35, f32[16,512,32]{1,2,0:T(8,128)} %copy.37, pred[16,512]{1,0:T(8,128)(4,1)S(1)} %get-tuple-element.21), kind=kLoop, calls=%fused_computation.6 | loop fusion | flops 16777216 | bytes 17833984 | tf_op jit(solution)/shard_map/convert_element_type | solution.py:121
  307.4 8.0 %convert_add_fusion.2 = (f32[16,64,512]{2,1,0:T(8,128)}, f32[16,64,512]{2,1,0:T(8,128)}) fusion(f32[16,64,512]{2,1,0:T(8,128)S(1)} %copy.27, f32[512]{0:T(512)S(1)} %mul.88, bf16[16,512,512]{1,2,0:T(8,128)(2,1)} %fusion, s32[16,512]{1,0:T(8,128)S(1)} %get-tuple-element.20), kind=kOutput, calls=%fused_computation.15 | convolution fusion | flops 539492352 | bytes 14714880 | tf_op jit(solution)/shard_map/tre,tec->trc/dot_general | solution.py:123
  334.5 8.2 %fusion.9 = f32[16,512,512]{2,1,0:T(8,128)} fusion(bf16[16,64,512]{1,0,2:T(8,128)(2,1)S(1)} %convert_element_type.93, s32[16,512]{1,0:T(8,128)S(1)} %get-tuple-element.20), kind=kOutput, calls=%fused_computation.23 | convolution fusion | flops 537395200 | bytes 17858560 | tf_op jit(solution)/shard_map/tre,trc->tec/dot_general | solution.py:54
  342.7 17.4 %copy.47 = f32[8192,512]{0,1:T(8,128)} copy(f32[8192,512]{1,0:T(8,128)} %bitcast.104) | data formatting | bytes 33554432 | tf_op jit(solution)/shard_map/reshape | solution.py:62
  360.1 17.8 %mul.105 = f32[8192,512]{0,1:T(8,128)} multiply(f32[8192,512]{0,1:T(8,128)} %copy.47, f32[8192,512]{0,1:T(8,128)} %bitcast.103) | non-fusion elementwise | flops 4194304 | bytes 50331648 | tf_op jit(solution)/shard_map/mul | solution.py:62
  378.0 17.4 %copy.48 = f32[8192,512]{1,0:T(8,128)} copy(f32[8192,512]{0,1:T(8,128)} %mul.105) | data formatting | bytes 33554432 | tf_op jit(solution)/shard_map/mul | solution.py:62
  395.4 52.9 %scatter_custom_fusion = f32[4097,512]{1,0:T(8,128)} fusion(s32[8192]{0:T(1024)S(1)} %bitcast.117, f32[8192,512]{1,0:T(8,128)} %copy.48, f32[]{:T(128)} %constant.12.clone.1), kind=kCustom, calls=%fused_computation.9 | custom fusion | flops 4194304 | bytes 8391168 | tf_op jit(solution)/shard_map/scatter-add | solution.py:68
  494.5 89.1 %all-reduce = (f32[1,32,32]{2,1,0:T(8,128)S(1)}, f32[1,32,32]{2,1,0:T(8,128)S(1)}, f32[1,32]{1,0:T(1,128)S(1)}, f32[1,32]{1,0:T(1,128)S(1)}) all-reduce(f32[1,32,32]{2,1,0:T(8,128)S(1)} %fusion.15, f32[1,32,32]{2,1,0:T(8,128)S(1)} %fusion.16, f32[1,32]{1,0:T(1,128)S(1)} %bitcast.119, ...), channel_id=1, replica_groups=mesh['node'=32,'query'=4] {'node','query'}, use_global_device_ids=true, to_apply=%region_2.5 | all-reduce | flops 2112 | bytes 16896 | tf_op jit(solution)/shard_map/psum | solution.py:73
  (102 shorter events, 116.2 us)
Async XLA Ops:
  0.6 75.5 %copy-start = (f32[822,32]{0,1:T(8,128)S(1)}, f32[822,32]{0,1:T(8,128)}, u32[]{:S(2)}) copy-start(f32[822,32]{0,1:T(8,128)} %param.17) | copy-start | bytes 315652
  0.6 116.4 %collective-permute-start.1 = (bf16[1024,512]{1,0:T(8,128)(2,1)}, bf16[1024,512]{1,0:T(8,128)(2,1)}, u32[]{:S(2)}, u32[]{:S(2)}) collective-permute-start(bf16[1024,512]{1,0:T(8,128)(2,1)} %param.13), channel_id=1, source_target_pairs={{4,0},{8,4},{12,8},{16,12},{20,16},{24,20},{28,24},{32,28},{36,32}... | collective-permute-start | bytes 3145736 | tf_op jit(solution)/shard_map/ppermute | solution.py:18
  10.1 106.9 %collective-permute-start = (bf16[1024,512]{1,0:T(8,128)(2,1)}, bf16[1024,512]{1,0:T(8,128)(2,1)}, u32[]{:S(2)}, u32[]{:S(2)}) collective-permute-start(bf16[1024,512]{1,0:T(8,128)(2,1)} %param.13), channel_id=1, source_target_pairs={{0,4},{4,8},{8,12},{12,16},{16,20},{20,24},{24,28},{28,32},{32,36}... | collective-permute-start | bytes 3145736 | tf_op jit(solution)/shard_map/ppermute | solution.py:15
  10.1 106.9 %collective-permute-start.2 = (bf16[1024,512]{1,0:T(8,128)(2,1)}, bf16[1024,512]{1,0:T(8,128)(2,1)}, u32[]{:S(2)}, u32[]{:S(2)}) collective-permute-start(bf16[1024,512]{1,0:T(8,128)(2,1)} %param.13), channel_id=1, source_target_pairs={{0,64},{64,0},{4,68},{68,4},{8,72},{72,8},{12,76},{76,12},{16,80},... | collective-permute-start | bytes 3145736 | tf_op jit(solution)/shard_map/ppermute | solution.py:30
  68.7 7.5 %copy-start.17 = (s32[16]{0:T(128)S(1)}, s32[16]{0:T(128)}, u32[]{:S(2)}) copy-start(s32[16]{0:T(128)} %param.16) | copy-start | bytes 196
  76.4 7.4 %copy-start.13 = (f32[16,32]{1,0:T(8,128)}, f32[16,32]{1,0:T(8,128)S(1)}, u32[]{:S(2)}) copy-start(f32[16,32]{1,0:T(8,128)S(1)} %fusion.24) | copy-start | bytes 6148
  80.1 3.7 copy-start.12
  80.2 3.8 copy-start.18
  99.2 17.8 %copy-start.16 = (f32[2,32]{1,0:T(2,128)S(1)}, f32[2,32]{1,0:T(2,128)}, u32[]{:S(2)}) copy-start(f32[2,32]{1,0:T(2,128)} %param.20) | copy-start | bytes 772
  99.3 17.8 %copy-start.9 = (bf16[1024,512]{1,0:T(8,128)(2,1)S(1)}, bf16[1024,512]{1,0:T(8,128)(2,1)}, u32[]{:S(2)}) copy-start(bf16[1024,512]{1,0:T(8,128)(2,1)} %param.13) | copy-start | bytes 3145732
  192.1 4.9 copy-start.15
  207.9 38.6 %copy-start.2 = (bf16[1024,512]{1,0:T(8,128)(2,1)}, bf16[1024,512]{1,0:T(8,128)(2,1)S(1)}, u32[]{:S(2)}) copy-start(bf16[1024,512]{1,0:T(8,128)(2,1)S(1)} %add_convert_fusion.1) | copy-start | bytes 3145732
  207.9 25.0 %collective-permute-start.5 = (bf16[1024,512]{1,0:T(8,128)(2,1)S(1)}, bf16[1024,512]{1,0:T(8,128)(2,1)S(1)}, u32[]{:S(2)}, u32[]{:S(2)}) collective-permute-start(bf16[1024,512]{1,0:T(8,128)(2,1)S(1)} %add_convert_fusion.1), channel_id=1, source_target_pairs={{0,64},{64,0},{4,68},{68,4},{8,72},{72,8},{12,76},{76,12},{16,80},... | collective-permute-start | bytes 3145736 | tf_op jit(solution)/shard_map/ppermute | solution.py:30
  210.9 27.9 %collective-permute-start.4 = (bf16[1024,512]{1,0:T(8,128)(2,1)S(1)}, bf16[1024,512]{1,0:T(8,128)(2,1)S(1)}, u32[]{:S(2)}, u32[]{:S(2)}) collective-permute-start(bf16[1024,512]{1,0:T(8,128)(2,1)S(1)} %add_convert_fusion.1), channel_id=1, source_target_pairs={{4,0},{8,4},{12,8},{16,12},{20,16},{24,20},{28,24},{32,28},{36,32}... | collective-permute-start | bytes 3145736 | tf_op jit(solution)/shard_map/ppermute | solution.py:18
  218.1 28.4 %collective-permute-start.3 = (bf16[1024,512]{1,0:T(8,128)(2,1)S(1)}, bf16[1024,512]{1,0:T(8,128)(2,1)S(1)}, u32[]{:S(2)}, u32[]{:S(2)}) collective-permute-start(bf16[1024,512]{1,0:T(8,128)(2,1)S(1)} %add_convert_fusion.1), channel_id=1, source_target_pairs={{0,4},{4,8},{8,12},{12,16},{16,20},{20,24},{24,28},{28,32},{32,36}... | collective-permute-start | bytes 3145736 | tf_op jit(solution)/shard_map/ppermute | solution.py:15
  452.2 3.4 copy-start.5
  454.1 26.9 %collective-permute-start.6 = (bf16[1024,512]{1,0:T(8,128)(2,1)}, bf16[1024,512]{1,0:T(8,128)(2,1)}, u32[]{:S(2)}, u32[]{:S(2)}) collective-permute-start(bf16[1024,512]{1,0:T(8,128)(2,1)} %get-tuple-element.13), channel_id=1, source_target_pairs={{4,0},{8,4},{12,8},{16,12},{20,16},{24,20},{28,24},{32,28},{36,32}... | collective-permute-start | bytes 3145736 | tf_op jit(solution)/shard_map/ppermute | solution.py:36
  454.3 26.6 %collective-permute-start.8 = (bf16[1024,512]{1,0:T(8,128)(2,1)}, bf16[1024,512]{1,0:T(8,128)(2,1)}, u32[]{:S(2)}, u32[]{:S(2)}) collective-permute-start(bf16[1024,512]{1,0:T(8,128)(2,1)} %get-tuple-element.14), channel_id=1, source_target_pairs={{0,64},{64,0},{4,68},{68,4},{8,72},{72,8},{12,76},{76,12},{16,80},... | collective-permute-start | bytes 3145736 | tf_op jit(solution)/shard_map/ppermute | solution.py:30
  454.4 27.5 %collective-permute-start.7 = (bf16[1024,512]{1,0:T(8,128)(2,1)}, bf16[1024,512]{1,0:T(8,128)(2,1)}, u32[]{:S(2)}, u32[]{:S(2)}) collective-permute-start(bf16[1024,512]{1,0:T(8,128)(2,1)} %get-tuple-element.15), channel_id=1, source_target_pairs={{124,0},{0,4},{4,8},{8,12},{12,16},{16,20},{20,24},{24,28},{28,32}... | collective-permute-start | bytes 3145736 | tf_op jit(solution)/shard_map/ppermute | solution.py:36
  470.8 5.0 copy-start.3
  470.8 8.0 %copy-start.11 = (f32[1024,16]{0,1:T(8,128)S(1)}, f32[1024,16]{0,1:T(8,128)}, u32[]{:S(2)}) copy-start(f32[1024,16]{0,1:T(8,128)} %copy-done.10) | copy-start | bytes 196612
  470.8 8.0 %copy-start.14 = (f32[16,32]{1,0:T(8,128)S(1)}, f32[16,32]{1,0:T(8,128)}, u32[]{:S(2)}) copy-start(f32[16,32]{1,0:T(8,128)} %copy-done.13) | copy-start | bytes 6148
  475.8 3.1 copy-start.7
  492.4 92.3 %copy-start.1 = (f32[822,32]{0,1:T(8,128)S(1)}, f32[822,32]{0,1:T(8,128)}, u32[]{:S(2)}) copy-start(f32[822,32]{0,1:T(8,128)} %param.17) | copy-start | bytes 315652
  (4 other events, 10.4 us)
where the time goes:
time: 595 us; the launch traced here: 585 us
  local copies, waits for them, and re-layouts  279 us (47%)
  other arithmetic  123 us (21%)
  blocking collectives  89.1 us (15%)
  matrix products  42 us (7%)
  waiting for transfers between devices  29.3 us (5%)
  starting transfers between devices  21.3 us (4%)
    gather x4, local copies, waits for them, and re-layouts, run_layer(): gathered = jnp.take(extended, edge_tiles[:, 0, :], axis=0)  97.8 us
    psum x1, blocking collectives, reduce_grads(): return lax.psum((values[0], values[1]), ('node', 'query'))  89.1 us
    gather x2, local copies, waits for them, and re-layouts, run_layer(): rel_scales = jnp.take(rel_vectors[layer_index], edge_tiles[:, 2, :], axis=0)  55.5 us
    scatter-add x1, other arithmetic, contributions(): jax.ops.segment_sum(edge_terms, segment_ids, num_segments=slot_count + 1)  52.9 us
    unnamed x46, local copies, waits for them, and re-layouts  23.4 us
    convert_element_type x2, other arithmetic, run_layer(): message = (gathered.reshape(tile_count, slot_total, query_count, DIM) * r...  19.4 us
    add x4, local copies, waits for them, and re-layouts, run_layer(): mixed_in = boundary.astype(jnp.float32) + summed  18 us
    mul x1, other arithmetic, contributions(): per_edge.reshape(tile_count, slot_total, col_count // DIM, DIM)  17.8 us
  transfers between devices with their start and end apart: 9, of which 4 were waited for; matrix products, arithmetic and copies ran while one was open for 23% of the time, Pallas kernels for 0%

commit v1 on v0

--- a/solution.py
+++ b/solution.py
@@ -70,7 +70,7 @@
 
 
 def reduce_grads(values):
-    return lax.psum((values[0], values[1]), ("node", "query"))
+    return lax.psum(lax.psum((values[0], values[1]), "query"), "node")
 
 
 def body(

time: 595 us -> 711 us (1.19)
  the two profiles are of different devices: /device:TPU:1 before, /device:TPU:0 now
where the time goes in v1:
time: 711 us; the launch traced here: 701 us
  local copies, waits for them, and re-layouts  279 us (39%)
  blocking collectives  202 us (28%)
  other arithmetic  121 us (17%)
  matrix products  44.4 us (6%)
  waiting for transfers between devices  29.9 us (4%)
  starting transfers between devices  22.8 us (3%)
    psum x2, blocking collectives, reduce_grads(): return lax.psum(lax.psum((values[0], values[1]), 'query'), 'node')  202 us
    gather x4, local copies, waits for them, and re-layouts, run_layer(): gathered = jnp.take(extended, edge_tiles[:, 0, :], axis=0)  98.1 us
    gather x2, local copies, waits for them, and re-layouts, run_layer(): rel_scales = jnp.take(rel_vectors[layer_index], edge_tiles[:, 2, :], axis=0)  55.8 us
    scatter-add x1, other arithmetic, contributions(): jax.ops.segment_sum(edge_terms, segment_ids, num_segments=slot_count + 1)  52.9 us
    unnamed x44, local copies, waits for them, and re-layouts  23.4 us
    convert_element_type x2, other arithmetic, run_layer(): message = (gathered.reshape(tile_count, slot_total, query_count, DIM) * r...  19.4 us
    add x4, local copies, waits for them, and re-layouts, run_layer(): mixed_in = boundary.astype(jnp.float32) + summed  18 us
    mul x1, other arithmetic, contributions(): per_edge.reshape(tile_count, slot_total, col_count // DIM, DIM)  17.8 us
  transfers between devices with their start and end apart: 9, of which 4 were waited for; matrix products, arithmetic and copies ran while one was open for 19% of the time, Pallas kernels for 0%

profile of v1, /device:TPU:0, one launch (start us, length us, event | category | flops | bytes accessed | tf_op | source)
XLA Modules:
  0.0 700.5 jit_solution(2573235852452395883)
XLA Ops:
  0.6 9.0 %collective-permute-start.1 = (bf16[1024,512]{1,0:T(8,128)(2,1)}, bf16[1024,512]{1,0:T(8,128)(2,1)}, u32[]{:S(2)}, u32[]{:S(2)}) collective-permute-start(bf16[1024,512]{1,0:T(8,128)(2,1)} %param.13), channel_id=1, source_target_pairs={{4,0},{8,4},{12,8},{16,12},{20,16},{24,20},{28,24},{32,28},{36,32}... | collective-permute-start | bytes 3145736 | tf_op jit(solution)/shard_map/ppermute | solution.py:18
  13.0 27.9 %gather_fusion.1 = f32[8192,32]{1,0:T(8,128)} fusion(f32[822,32]{1,0:T(8,128)S(1)} %bitcast.102, s32[8192]{0:T(1024)S(1)} %broadcast_clamp_fusion), kind=kCustom, calls=%fused_computation.1.clone | custom fusion | bytes 2129920 | tf_op jit(solution)/shard_map/jit(_take)/gather | solution.py:118
  40.9 27.9 %gather_fusion.3 = f32[8192,32]{1,0:T(8,128)} fusion(f32[822,32]{1,0:T(8,128)S(1)} %bitcast.101, s32[8192]{0:T(1024)S(1)} %broadcast_clamp_fusion), kind=kCustom, calls=%fused_computation.3.clone | custom fusion | bytes 2129920 | tf_op jit(solution)/shard_map/jit(_take)/gather | solution.py:118
  68.7 7.4 %broadcast_select_fusion = (f32[16,512,32]{2,1,0:T(8,128)}, f32[16,512,32]{2,1,0:T(8,128)}) fusion(f32[16,512,32]{2,1,0:T(8,128)} %bitcast.109, pred[16,512]{1,0:T(8,128)(4,1)S(1)} %get-tuple-element.26, f32[16,512,32]{2,1,0:T(8,128)} %bitcast.108), kind=kLoop, calls=%fused_computation.25 | loop fusion | flops 524288 | bytes 4202496 | tf_op jit(solution)/shard_map/jit(_take)/select_n | solution.py:118
  99.3 17.7 %copy.64 = f32[64,8,16,512]{3,1,2,0:T(8,128)} copy(f32[64,8,16,512]{3,2,1,0:T(8,128)S(1)} %bitcast.105) | data formatting | bytes 33554432
  120.6 36.7 %gather_fusion = bf16[8192,512]{1,0:T(8,128)(2,1)} fusion(bf16[4096,512]{1,0:T(8,128)(2,1)} %pad_maximum_fusion, s32[8192]{0:T(1024)S(1)} %broadcast_clamp_fusion.1), kind=kCustom, calls=%fused_computation.clone | custom fusion | bytes 16809984 | tf_op jit(solution)/shard_map/jit(_take)/gather | solution.py:117
  157.3 12.5 %copy.28 = bf16[16,512,512]{1,2,0:T(8,128)(2,1)} copy(bf16[16,512,512]{2,1,0:T(8,128)(2,1)} %bitcast.107) | data formatting | bytes 16777216 | tf_op jit(solution)/shard_map/jit(_take)/gather | solution.py:117
  169.7 9.7 %fusion.1 = bf16[16,512,512]{1,2,0:T(8,128)(2,1)} fusion(bf16[16,512,512]{1,2,0:T(8,128)(2,1)} %copy.28, f32[16,512,32]{1,2,0:T(8,128)} %copy.30, pred[16,512]{1,0:T(8,128)(4,1)S(1)} %get-tuple-element.25), kind=kLoop, calls=%fused_computation.8 | loop fusion | flops 16777216 | bytes 17833984 | tf_op jit(solution)/shard_map/convert_element_type | solution.py:121
  179.4 8.0 %convert_add_fusion.3 = (f32[16,64,512]{2,1,0:T(8,128)}, f32[16,64,512]{2,1,0:T(8,128)}) fusion(f32[16,64,512]{2,1,0:T(8,128)S(1)} %copy.27, f32[512]{0:T(512)S(1)} %mul.88, bf16[16,512,512]{1,2,0:T(8,128)(2,1)} %fusion.1, s32[16,512]{1,0:T(8,128)S(1)} %get-tuple-element.24), kind=kOutput, calls=%fused_computation.16 | convolution fusion | flops 539492352 | bytes 14714880 | tf_op jit(solution)/shard_map/tre,tec->trc/dot_general | solution.py:123
  211.4 7.7 %collective-permute-start.4 = (bf16[1024,512]{1,0:T(8,128)(2,1)S(1)}, bf16[1024,512]{1,0:T(8,128)(2,1)S(1)}, u32[]{:S(2)}, u32[]{:S(2)}) collective-permute-start(bf16[1024,512]{1,0:T(8,128)(2,1)S(1)} %add_convert_fusion.1), channel_id=1, source_target_pairs={{4,0},{8,4},{12,8},{16,12},{20,16},{24,20},{28,24},{32,28},{36,32}... | collective-permute-start | bytes 3145736 | tf_op jit(solution)/shard_map/ppermute | solution.py:18
  219.2 14.9 %collective-permute-done.5 = bf16[1024,512]{1,0:T(8,128)(2,1)S(1)} collective-permute-done((bf16[1024,512]{1,0:T(8,128)(2,1)S(1)}, bf16[1024,512]{1,0:T(8,128)(2,1)S(1)}, u32[]{:S(2)}, u32[]{:S(2)}) %collective-permute-start.5) | collective-permute-done | bytes 1048608 | tf_op jit(solution)/shard_map/ppermute | solution.py:30
  234.1 6.4 collective-permute-done.4
  240.5 8.0 %collective-permute-done.3 = bf16[1024,512]{1,0:T(8,128)(2,1)S(1)} collective-permute-done((bf16[1024,512]{1,0:T(8,128)(2,1)S(1)}, bf16[1024,512]{1,0:T(8,128)(2,1)S(1)}, u32[]{:S(2)}, u32[]{:S(2)}) %collective-permute-start.3) | collective-permute-done | bytes 1048608 | tf_op jit(solution)/shard_map/ppermute | solution.py:15
  250.9 36.7 %gather_fusion.2 = bf16[8192,512]{1,0:T(8,128)(2,1)} fusion(bf16[4096,512]{1,0:T(8,128)(2,1)} %pad_maximum_fusion.1, s32[8192]{0:T(1024)S(1)} %broadcast_clamp_fusion.1), kind=kCustom, calls=%fused_computation.2.clone | custom fusion | bytes 16809984 | tf_op jit(solution)/shard_map/jit(_take)/gather | solution.py:117
  287.5 12.3 %copy.35 = bf16[16,512,512]{1,2,0:T(8,128)(2,1)} copy(bf16[16,512,512]{2,1,0:T(8,128)(2,1)} %bitcast.106) | data formatting | bytes 16777216 | tf_op jit(solution)/shard_map/jit(_take)/gather | solution.py:117
  299.9 9.7 %fusion = bf16[16,512,512]{1,2,0:T(8,128)(2,1)} fusion(bf16[16,512,512]{1,2,0:T(8,128)(2,1)} %copy.35, f32[16,512,32]{1,2,0:T(8,128)} %copy.37, pred[16,512]{1,0:T(8,128)(4,1)S(1)} %get-tuple-element.25), kind=kLoop, calls=%fused_computation.6 | loop fusion | flops 16777216 | bytes 17833984 | tf_op jit(solution)/shard_map/convert_element_type | solution.py:121
  309.5 8.0 %convert_add_fusion.2 = (f32[16,64,512]{2,1,0:T(8,128)}, f32[16,64,512]{2,1,0:T(8,128)}) fusion(f32[16,64,512]{2,1,0:T(8,128)S(1)} %copy.27, f32[512]{0:T(512)S(1)} %mul.88, bf16[16,512,512]{1,2,0:T(8,128)(2,1)} %fusion, s32[16,512]{1,0:T(8,128)S(1)} %get-tuple-element.24), kind=kOutput, calls=%fused_computation.15 | convolution fusion | flops 539492352 | bytes 14714880 | tf_op jit(solution)/shard_map/tre,tec->trc/dot_general | solution.py:123
  336.7 8.2 %fusion.9 = f32[16,512,512]{2,1,0:T(8,128)} fusion(bf16[16,64,512]{1,0,2:T(8,128)(2,1)S(1)} %convert_element_type.93, s32[16,512]{1,0:T(8,128)S(1)} %get-tuple-element.24), kind=kOutput, calls=%fused_computation.23 | convolution fusion | flops 537395200 | bytes 17858560 | tf_op jit(solution)/shard_map/tre,trc->tec/dot_general | solution.py:54
  344.9 17.4 %copy.47 = f32[8192,512]{0,1:T(8,128)} copy(f32[8192,512]{1,0:T(8,128)} %bitcast.104) | data formatting | bytes 33554432 | tf_op jit(solution)/shard_map/reshape | solution.py:62
  362.3 17.8 %mul.105 = f32[8192,512]{0,1:T(8,128)} multiply(f32[8192,512]{0,1:T(8,128)} %copy.47, f32[8192,512]{0,1:T(8,128)} %bitcast.103) | non-fusion elementwise | flops 4194304 | bytes 50331648 | tf_op jit(solution)/shard_map/mul | solution.py:62
  380.1 17.4 %copy.48 = f32[8192,512]{1,0:T(8,128)} copy(f32[8192,512]{0,1:T(8,128)} %mul.105) | data formatting | bytes 33554432 | tf_op jit(solution)/shard_map/mul | solution.py:62
  397.6 52.9 %scatter_custom_fusion = f32[4097,512]{1,0:T(8,128)} fusion(s32[8192]{0:T(1024)S(1)} %bitcast.117, f32[8192,512]{1,0:T(8,128)} %copy.48, f32[]{:T(128)} %constant.12.clone.1), kind=kCustom, calls=%fused_computation.9 | custom fusion | flops 4194304 | bytes 8391168 | tf_op jit(solution)/shard_map/scatter-add | solution.py:68
  497.4 10.5 %all-reduce.1 = (f32[32,32]{1,0:T(8,128)S(1)}, f32[32,32]{1,0:T(8,128)S(1)}, f32[32]{0:T(128)S(1)}, f32[32]{0:T(128)S(1)}) all-reduce(f32[32,32]{1,0:T(8,128)S(1)} %fusion.15, f32[32,32]{1,0:T(8,128)S(1)} %fusion.16, f32[32]{0:T(128)S(1)} %get-tuple-element.15, ...), channel_id=1, replica_groups=mesh['node'=32,'query'=4] {'query'}, use_global_device_ids=true, to_apply=%region_3.6 | all-reduce | flops 2112 | bytes 16896 | tf_op jit(solution)/shard_map/psum | solution.py:73
  507.9 191.2 %all-reduce = (f32[1,32,32]{2,1,0:T(8,128)S(1)}, f32[1,32,32]{2,1,0:T(8,128)S(1)}, f32[1,32]{1,0:T(1,128)S(1)}, f32[1,32]{1,0:T(1,128)S(1)}) all-reduce(f32[1,32,32]{2,1,0:T(8,128)S(1)} %bitcast.118, f32[1,32,32]{2,1,0:T(8,128)S(1)} %bitcast.119, f32[1,32]{1,0:T(1,128)S(1)} %bitcast.120, ...), channel_id=1, replica_groups=mesh['node'=32,'query'=4] {'node'}, use_global_device_ids=true, to_apply=%region_4.7 | all-reduce | flops 2112 | bytes 16896 | tf_op jit(solution)/shard_map/psum | solution.py:73
  (101 shorter events, 123.5 us)
Async XLA Ops:
  0.6 75.5 %copy-start = (f32[822,32]{0,1:T(8,128)S(1)}, f32[822,32]{0,1:T(8,128)}, u32[]{:S(2)}) copy-start(f32[822,32]{0,1:T(8,128)} %param.17) | copy-start | bytes 315652
  0.6 116.4 %collective-permute-start.1 = (bf16[1024,512]{1,0:T(8,128)(2,1)}, bf16[1024,512]{1,0:T(8,128)(2,1)}, u32[]{:S(2)}, u32[]{:S(2)}) collective-permute-start(bf16[1024,512]{1,0:T(8,128)(2,1)} %param.13), channel_id=1, source_target_pairs={{4,0},{8,4},{12,8},{16,12},{20,16},{24,20},{28,24},{32,28},{36,32}... | collective-permute-start | bytes 3145736 | tf_op jit(solution)/shard_map/ppermute | solution.py:18
  9.7 107.4 %collective-permute-start = (bf16[1024,512]{1,0:T(8,128)(2,1)}, bf16[1024,512]{1,0:T(8,128)(2,1)}, u32[]{:S(2)}, u32[]{:S(2)}) collective-permute-start(bf16[1024,512]{1,0:T(8,128)(2,1)} %param.13), channel_id=1, source_target_pairs={{0,4},{4,8},{8,12},{12,16},{16,20},{20,24},{24,28},{28,32},{32,36}... | collective-permute-start | bytes 3145736 | tf_op jit(solution)/shard_map/ppermute | solution.py:15
  9.7 107.4 %collective-permute-start.2 = (bf16[1024,512]{1,0:T(8,128)(2,1)}, bf16[1024,512]{1,0:T(8,128)(2,1)}, u32[]{:S(2)}, u32[]{:S(2)}) collective-permute-start(bf16[1024,512]{1,0:T(8,128)(2,1)} %param.13), channel_id=1, source_target_pairs={{0,64},{64,0},{4,68},{68,4},{8,72},{72,8},{12,76},{76,12},{16,80},... | collective-permute-start | bytes 3145736 | tf_op jit(solution)/shard_map/ppermute | solution.py:30
  68.7 7.4 %copy-start.16 = (s32[16]{0:T(128)S(1)}, s32[16]{0:T(128)}, u32[]{:S(2)}) copy-start(s32[16]{0:T(128)} %param.16) | copy-start | bytes 196
  76.4 7.4 %copy-start.12 = (f32[16,32]{1,0:T(8,128)}, f32[16,32]{1,0:T(8,128)S(1)}, u32[]{:S(2)}) copy-start(f32[16,32]{1,0:T(8,128)S(1)} %fusion.24) | copy-start | bytes 6148
  80.2 3.7 copy-start.11
  80.2 3.8 copy-start.17
  99.3 17.7 %copy-start.15 = (f32[2,32]{1,0:T(2,128)S(1)}, f32[2,32]{1,0:T(2,128)}, u32[]{:S(2)}) copy-start(f32[2,32]{1,0:T(2,128)} %param.20) | copy-start | bytes 772
  99.3 17.8 %copy-start.8 = (bf16[1024,512]{1,0:T(8,128)(2,1)S(1)}, bf16[1024,512]{1,0:T(8,128)(2,1)}, u32[]{:S(2)}) copy-start(bf16[1024,512]{1,0:T(8,128)(2,1)} %param.13) | copy-start | bytes 3145732
  192.3 4.9 copy-start.14
  208.2 40.4 %copy-start.2 = (bf16[1024,512]{1,0:T(8,128)(2,1)}, bf16[1024,512]{1,0:T(8,128)(2,1)S(1)}, u32[]{:S(2)}) copy-start(bf16[1024,512]{1,0:T(8,128)(2,1)S(1)} %add_convert_fusion.1) | copy-start | bytes 3145732
  208.2 25.9 %collective-permute-start.5 = (bf16[1024,512]{1,0:T(8,128)(2,1)S(1)}, bf16[1024,512]{1,0:T(8,128)(2,1)S(1)}, u32[]{:S(2)}, u32[]{:S(2)}) collective-permute-start(bf16[1024,512]{1,0:T(8,128)(2,1)S(1)} %add_convert_fusion.1), channel_id=1, source_target_pairs={{0,64},{64,0},{4,68},{68,4},{8,72},{72,8},{12,76},{76,12},{16,80},... | collective-permute-start | bytes 3145736 | tf_op jit(solution)/shard_map/ppermute | solution.py:30
  211.4 29.1 %collective-permute-start.4 = (bf16[1024,512]{1,0:T(8,128)(2,1)S(1)}, bf16[1024,512]{1,0:T(8,128)(2,1)S(1)}, u32[]{:S(2)}, u32[]{:S(2)}) collective-permute-start(bf16[1024,512]{1,0:T(8,128)(2,1)S(1)} %add_convert_fusion.1), channel_id=1, source_target_pairs={{4,0},{8,4},{12,8},{16,12},{20,16},{24,20},{28,24},{32,28},{36,32}... | collective-permute-start | bytes 3145736 | tf_op jit(solution)/shard_map/ppermute | solution.py:18
  219.2 29.3 %collective-permute-start.3 = (bf16[1024,512]{1,0:T(8,128)(2,1)S(1)}, bf16[1024,512]{1,0:T(8,128)(2,1)S(1)}, u32[]{:S(2)}, u32[]{:S(2)}) collective-permute-start(bf16[1024,512]{1,0:T(8,128)(2,1)S(1)} %add_convert_fusion.1), channel_id=1, source_target_pairs={{0,4},{4,8},{8,12},{12,16},{16,20},{20,24},{24,28},{28,32},{32,36}... | collective-permute-start | bytes 3145736 | tf_op jit(solution)/shard_map/ppermute | solution.py:15
  454.4 4.0 copy-start.4
  456.0 28.2 %collective-permute-start.6 = (bf16[1024,512]{1,0:T(8,128)(2,1)}, bf16[1024,512]{1,0:T(8,128)(2,1)}, u32[]{:S(2)}, u32[]{:S(2)}) collective-permute-start(bf16[1024,512]{1,0:T(8,128)(2,1)} %get-tuple-element.17), channel_id=1, source_target_pairs={{4,0},{8,4},{12,8},{16,12},{20,16},{24,20},{28,24},{32,28},{36,32}... | collective-permute-start | bytes 3145736 | tf_op jit(solution)/shard_map/ppermute | solution.py:36
  456.3 27.9 %collective-permute-start.8 = (bf16[1024,512]{1,0:T(8,128)(2,1)}, bf16[1024,512]{1,0:T(8,128)(2,1)}, u32[]{:S(2)}, u32[]{:S(2)}) collective-permute-start(bf16[1024,512]{1,0:T(8,128)(2,1)} %get-tuple-element.18), channel_id=1, source_target_pairs={{0,64},{64,0},{4,68},{68,4},{8,72},{72,8},{12,76},{76,12},{16,80},... | collective-permute-start | bytes 3145736 | tf_op jit(solution)/shard_map/ppermute | solution.py:30
  456.7 28.2 %collective-permute-start.7 = (bf16[1024,512]{1,0:T(8,128)(2,1)S(1)}, bf16[1024,512]{1,0:T(8,128)(2,1)}, u32[]{:S(2)}, u32[]{:S(2)}) collective-permute-start(bf16[1024,512]{1,0:T(8,128)(2,1)S(1)} %get-tuple-element.19), channel_id=1, source_target_pairs={{124,0},{0,4},{4,8},{8,12},{12,16},{16,20},{20,24},{24,28},{28,32}... | collective-permute-start | bytes 3145736 | tf_op jit(solution)/shard_map/ppermute | solution.py:36
  473.6 4.9 copy-start.10
  473.6 4.9 copy-start.13
  478.5 4.4 copy-start.3
  478.5 4.4 copy-start.6
  495.4 204.9 %copy-start.1 = (f32[822,32]{0,1:T(8,128)S(1)}, f32[822,32]{0,1:T(8,128)}, u32[]{:S(2)}) copy-start(f32[822,32]{0,1:T(8,128)} %param.17) | copy-start | bytes 315652
  (3 other events, 6.2 us)
